TPU v7x, 512 devices: a whole 4x8x8 slice. The times are simulated.
512 devices in a mesh: dp: 8 (over z), expert: 64 (over x, y, core).
Axes of the slice: x: 4, y: 8, z: 8, core: 2. Of those that a mesh axis runs over, the one named last changes fastest.
Arguments:
- tokens: bfloat16 [65536, 1024], P(('dp', 'expert')), may hold values from -6 to 6
- d_output: bfloat16 [65536, 1024], P(('dp', 'expert')), may hold values from -6 to 6
- combine: float32 [65536, 8], P(('dp', 'expert')), may hold values from 0.05 to 1
- routes: int32 [65536, 8], P(('dp', 'expert')), may hold values from 0 to 63, all different within a row; in each aligned block of 128 rows (0 to 127, 128 to 255, ...) at most 18 rows name the same one
- gate_weight: bfloat16 [64, 1024, 384], P('expert', 'dp'), may hold values from -0.1875 to 0.1875
- up_weight: bfloat16 [64, 1024, 384], P('expert', 'dp'), may hold values from -0.1875 to 0.1875
- down_weight: bfloat16 [64, 384, 1024], P('expert', None, 'dp'), may hold values from -0.3125 to 0.3125
Outputs:
- d_tokens: bfloat16 [65536, 1024], P(('dp', 'expert'))
- d_gate_weight: float32 [64, 1024, 384], P('expert', 'dp')
- d_up_weight: float32 [64, 1024, 384], P('expert', 'dp')
- d_down_weight: float32 [64, 384, 1024], P('expert', None, 'dp')
Inputs may be any that keep to these rules, and one draw needn't show every extreme that they name: `routes`: among the 128 tokens of one device, each expert id is named by at most 18 rows; some expert is named by exactly 18 rows on some device. The ids of one token differ.
All inputs are finite; a program needn't handle non-finite values.
Results may differ from a plain program's by a relative error of at most 0.015.
Values may be sent and summed in bfloat16 or wider, within the bound.
A program may use at most 64 MiB of HBM per device.

v0:
```python
import jax
import jax.numpy as jnp
from jax import lax
from jax.sharding import PartitionSpec as P


def route_slots(routes, experts):
    matches = (routes[:, :, None] == jnp.arange(experts, dtype=jnp.int32)[None, None, :]).astype(
        jnp.int32
    )
    per_token = jnp.sum(matches, axis=1)
    tok_count = per_token.shape[0]
    before = jnp.tri(tok_count, k=-1, dtype=jnp.bfloat16)
    earlier = jnp.dot(
        before, per_token.astype(jnp.bfloat16), preferred_element_type=jnp.float32
    ).astype(jnp.int32)
    return jnp.sum(matches * earlier[:, None, :], axis=2)


def row_work(row_inputs, row_grads, gate_up, down_matrix):
    hidden_units = down_matrix.shape[0]
    preact = jnp.dot(row_inputs, gate_up, preferred_element_type=jnp.float32)
    gate_pre = preact[:, :hidden_units]
    up_pre = preact[:, hidden_units:]
    gate_sigmoid = jax.nn.sigmoid(gate_pre)
    hidden = (gate_pre * gate_sigmoid * up_pre).astype(jnp.bfloat16)
    d_hidden = jnp.dot(row_grads, down_matrix.T, preferred_element_type=jnp.float32)
    d_gate_pre = d_hidden * up_pre * gate_sigmoid * (1.0 + gate_pre * (1.0 - gate_sigmoid))
    d_up_pre = d_hidden * gate_pre * gate_sigmoid
    d_preact = jnp.concatenate([d_gate_pre, d_up_pre], axis=1).astype(jnp.bfloat16)
    d_rows = jnp.dot(d_preact, gate_up.T, preferred_element_type=jnp.float32).astype(jnp.bfloat16)
    return (d_rows, hidden, d_preact)


def body(tokens, d_output, combine, routes, gate_weight, up_weight, down_weight):
    experts = lax.axis_size("expert")
    tok_count = tokens.shape[0]
    model_width = tokens.shape[1]
    top_count = routes.shape[1]
    capacity = max(2, (9 * tok_count * top_count + 8 * experts - 1) // (8 * experts))
    slot_count = experts * capacity
    slot_index = route_slots(routes, experts)
    position = (routes * capacity + slot_index).reshape(-1)
    spread_inputs = jnp.repeat(tokens, top_count, axis=0)
    scaled = (
        (combine[:, :, None] * d_output[:, None, :].astype(jnp.float32))
        .astype(jnp.bfloat16)
        .reshape(-1, model_width)
    )
    send_inputs = (
        jnp.zeros((slot_count, model_width), jnp.bfloat16)
        .at[position]
        .set(spread_inputs)
        .reshape(experts, capacity, model_width)
    )
    send_grads = (
        jnp.zeros((slot_count, model_width), jnp.bfloat16)
        .at[position]
        .set(scaled)
        .reshape(experts, capacity, model_width)
    )
    whole_gate, whole_up, whole_down = (
        lax.all_gather(gate_weight, "dp", axis=1, tiled=True),
        lax.all_gather(up_weight, "dp", axis=1, tiled=True),
        lax.all_gather(down_weight, "dp", axis=2, tiled=True),
    )
    gate_up = jnp.concatenate([whole_gate[0], whole_up[0]], axis=1)
    down_matrix = whole_down[0]
    hidden_units = down_matrix.shape[0]
    recv_inputs, recv_grads = (
        lax.all_to_all(send_inputs, "expert", split_axis=0, concat_axis=0, tiled=True),
        lax.all_to_all(send_grads, "expert", split_axis=0, concat_axis=0, tiled=True),
    )
    flat_inputs = recv_inputs.reshape(-1, model_width)
    flat_grads = recv_grads.reshape(-1, model_width)
    d_rows, hidden, d_preact = row_work(flat_inputs, flat_grads, gate_up, down_matrix)
    returned = lax.all_to_all(
        d_rows.reshape(experts, capacity, model_width),
        "expert",
        split_axis=0,
        concat_axis=0,
        tiled=True,
    )
    route_rows = returned.reshape(-1, model_width)[position].reshape(
        tok_count, top_count, model_width
    )
    d_tokens = jnp.sum(route_rows.astype(jnp.float32), axis=1).astype(jnp.bfloat16)
    gate_up_grad = jnp.dot(flat_inputs.T, d_preact, preferred_element_type=jnp.float32)
    down_grad = jnp.dot(flat_grads.T, hidden, preferred_element_type=jnp.float32)
    stacked = jnp.concatenate([gate_up_grad, down_grad], axis=1)
    summed = lax.psum_scatter(
        stacked.astype(jnp.bfloat16), "dp", scatter_dimension=0, tiled=True
    ).astype(jnp.float32)
    d_gate_weight = summed[:, :hidden_units][None]
    d_up_weight = summed[:, hidden_units : 2 * hidden_units][None]
    d_down_weight = summed[:, 2 * hidden_units :].T[None]
    return (d_tokens, d_gate_weight, d_up_weight, d_down_weight)


def solution(mesh):
    placed = (
        P(("dp", "expert"), None),
        P(("dp", "expert"), None),
        P(("dp", "expert"), None),
        P(("dp", "expert"), None),
        P("expert", "dp", None),
        P("expert", "dp", None),
        P("expert", None, "dp"),
    )
    return jax.shard_map(
        body,
        mesh=mesh,
        in_specs=placed,
        out_specs=(
            P(("dp", "expert"), None),
            P("expert", "dp", None),
            P("expert", "dp", None),
            P("expert", None, "dp"),
        ),
        check_vma=False,
    )
```

profile of v0, /device:TPU:1, one launch (start us, length us, event | category | flops | bytes accessed | tf_op | source)
XLA Modules:
  0.0 330.3 jit_solution(3674698657693354905)
XLA Ops:
  7.2 0.8 convert_reduce_fusion
  8.2 0.7 select_reduce_fusion
  9.8 6.0 %scatter_custom_fusion.1 = bf16[1152,1024]{1,0:T(8,128)(2,1)S(1)} fusion(s32[1024]{0:T(1024)S(1)} %bitcast.37, bf16[]{:T(256)} %constant.6.clone.1, bf16[128,1024]{1,0:T(8,128)(2,1)S(1)} %copy-done), kind=kCustom, calls=%fused_computation.9 | custom fusion | bytes 2621442 | tf_op jit(solution)/shard_map/scatter | solution.py:53
  15.9 2.4 reshape.76
  18.3 11.8 %all-to-all-start.1 = ((bf16[64,18,1024]{2,1,0:T(8,128)(2,1)}), bf16[64,18,1024]{2,1,0:T(8,128)(2,1)S(1)}, u32[]{:S(2)}, u32[]{:S(2)}) async-start(bf16[64,18,1024]{2,1,0:T(8,128)(2,1)} %reshape.76), calls=%async_computation.1 | async-start | bytes 6291456 | tf_op jit(solution)/shard_map/all_to_all | solution.py:71
  30.2 1.8 convert_element_type.34
  32.0 7.7 %scatter_custom_fusion = bf16[1152,1024]{1,0:T(8,128)(2,1)} fusion(s32[1024]{0:T(1024)S(1)} %bitcast.38, f32[128,1024]{1,0:T(8,128)} %convert_element_type.34, f32[1024]{0:T(1024)S(1)} %mul.60, bf16[]{:T(256)} %constant.6.clone.1), kind=kCustom, calls=%fused_computation.7 | custom fusion | flops 2097152 | bytes 2887682 | tf_op jit(solution)/shard_map/scatter | solution.py:59
  39.7 4.3 %reshape.73 = bf16[64,18,1024]{2,1,0:T(8,128)(2,1)} reshape(bf16[1152,1024]{1,0:T(8,128)(2,1)} %scatter_custom_fusion) | data formatting | bytes 4718592 | tf_op jit(solution)/shard_map/reshape | solution.py:60
  44.1 59.5 %all-to-all-done.1 = bf16[64,18,1024]{2,1,0:T(8,128)(2,1)S(1)} async-done(((bf16[64,18,1024]{2,1,0:T(8,128)(2,1)}), bf16[64,18,1024]{2,1,0:T(8,128)(2,1)S(1)}, u32[]{:S(2)}, u32[]{:S(2)}) %all-to-all-start.1) | async-done | bytes 2359328 | tf_op jit(solution)/shard_map/all_to_all | solution.py:71
  103.5 6.2 %all-to-all-start = ((bf16[64,18,1024]{2,1,0:T(8,128)(2,1)}), bf16[64,18,1024]{2,1,0:T(8,128)(2,1)}, u32[]{:S(2)}, u32[]{:S(2)}) async-start(bf16[64,18,1024]{2,1,0:T(8,128)(2,1)} %reshape.73), calls=%async_computation | async-start | bytes 6291456 | tf_op jit(solution)/shard_map/all_to_all | solution.py:72
  109.8 30.3 %all_gather.10 = bf16[1,1024,384]{2,1,0:T(8,128)(2,1)} all-gather(bf16[1,128,384]{2,1,0:T(8,128)(2,1)S(1)} %copy-done.5), channel_id=1, replica_groups=mesh['dp'=8,'expert'=64] {'dp'}, dimensions={1}, use_global_device_ids=true | all-gather | bytes 884736 | tf_op jit(solution)/shard_map/all_gather | solution.py:63
  140.1 24.1 %all_gather.11 = bf16[1,1024,384]{2,1,0:T(8,128)(2,1)} all-gather(bf16[1,128,384]{2,1,0:T(8,128)(2,1)} %param.12), channel_id=1, replica_groups=mesh['dp'=8,'expert'=64] {'dp'}, dimensions={1}, use_global_device_ids=true | all-gather | bytes 884736 | tf_op jit(solution)/shard_map/all_gather | solution.py:64
  164.2 22.5 %all_gather.9 = bf16[1,384,1024]{2,1,0:T(8,128)(2,1)} all-gather(bf16[1,384,128]{2,1,0:T(8,128)(2,1)} %param.13), channel_id=1, replica_groups=mesh['dp'=8,'expert'=64] {'dp'}, dimensions={2}, use_global_device_ids=true | all-gather | bytes 884736 | tf_op jit(solution)/shard_map/all_gather | solution.py:65
  186.7 2.2 reshape.77
  188.9 6.1 %fusion.10 = f32[1152,768]{0,1:T(8,128)} fusion(bf16[1152,1024]{1,0:T(8,128)(2,1)} %reshape.77, bf16[1024,384]{1,0:T(8,128)(2,1)} %bitcast.35, bf16[1024,384]{1,0:T(8,128)(2,1)} %bitcast.33), kind=kOutput, calls=%fused_computation.25 | convolution fusion | flops 1815085056 | bytes 7471104 | tf_op jit(solution)/shard_map/dot_general | solution.py:22
  195.0 2.9 reshape.74
  197.9 3.4 %convolution_convert_fusion.2 = bf16[1024,384]{0,1:T(8,128)(2,1)S(1)} fusion(bf16[1152,1024]{1,0:T(8,128)(2,1)S(1)} %reshape.74, f32[1152,768]{0,1:T(8,128)} %fusion.10), kind=kOutput, calls=%fused_computation.20 | convolution fusion | flops 909017088 | bytes 6684672 | tf_op jit(solution)/shard_map/dot_general | solution.py:89
  201.4 1.6 multiply_convert_fusion.2
  203.0 3.3 %convolution_convert_fusion.1 = bf16[1024,768]{0,1:T(8,128)(2,1)} fusion(bf16[1152,1024]{1,0:T(8,128)(2,1)S(1)} %copy-done.1, bf16[1152,384]{0,1:T(8,128)(2,1)S(1)} %get-tuple-element.21, bf16[1152,384]{0,1:T(8,128)(2,1)S(1)} %get-tuple-element.20), kind=kOutput, calls=%fused_computation.18 | convolution fusion | flops 1816264704 | bytes 5701632 | tf_op jit(solution)/shard_map/dot_general | solution.py:88
  206.4 2.1 convolution_convert_fusion
  208.5 2.4 reshape.78
  210.9 23.6 %all-to-all-start.2 = ((bf16[64,18,1024]{2,1,0:T(8,128)(2,1)}), bf16[64,18,1024]{2,1,0:T(8,128)(2,1)}, u32[]{:S(2)}, u32[]{:S(2)}) async-start(bf16[64,18,1024]{2,1,0:T(8,128)(2,1)} %reshape.78), calls=%async_computation.2 | async-start | bytes 6291456 | tf_op jit(solution)/shard_map/all_to_all | solution.py:77
  234.8 1.6 pad_maximum_fusion
  236.4 2.6 copy.31
  239.0 68.9 %all-to-all-done.2 = bf16[64,18,1024]{2,1,0:T(8,128)(2,1)} async-done(((bf16[64,18,1024]{2,1,0:T(8,128)(2,1)}), bf16[64,18,1024]{2,1,0:T(8,128)(2,1)}, u32[]{:S(2)}, u32[]{:S(2)}) %all-to-all-start.2) | async-done | bytes 2359328 | tf_op jit(solution)/shard_map/all_to_all | solution.py:77
  307.9 2.9 reshape.79
  310.9 5.3 %gather_fusion = bf16[1024,1024]{1,0:T(8,128)(2,1)} fusion(bf16[1152,1024]{1,0:T(8,128)(2,1)S(1)} %reshape.79, s32[1024]{0:T(1024)S(1)} %broadcast_clamp_fusion), kind=kCustom, calls=%fused_computation | custom fusion | bytes 4198400 | tf_op jit(solution)/shard_map/gather | solution.py:84
  316.2 3.7 %bitcast_reduce_fusion = bf16[128,1024]{1,0:T(8,128)(2,1)} fusion(bf16[1024,1024]{1,0:T(8,128)(2,1)} %gather_fusion), kind=kLoop, calls=%fused_computation.8 | loop fusion | flops 917504 | bytes 2359296 | tf_op jit(solution)/shard_map/reduce_sum | solution.py:87
  319.9 1.2 copy.32
  321.2 0.7 slice_bitcast_fusion
  321.9 0.8 copy.30
  322.7 0.8 copy.29
  (30 shorter events, 1.7 us)
Async XLA Ops:
  7.2 2.7 copy-start
  18.3 11.8 %copy-start.6 = (f32[128,8]{0,1:T(8,128)S(1)}, f32[128,8]{0,1:T(8,128)}, u32[]{:S(2)}) copy-start(f32[128,8]{0,1:T(8,128)} %param.9) | copy-start | bytes 12292
  18.3 85.3 %all-to-all-start.1 = ((bf16[64,18,1024]{2,1,0:T(8,128)(2,1)}), bf16[64,18,1024]{2,1,0:T(8,128)(2,1)S(1)}, u32[]{:S(2)}, u32[]{:S(2)}) async-start(bf16[64,18,1024]{2,1,0:T(8,128)(2,1)} %reshape.76), calls=%async_computation.1 | async-start | bytes 6291456 | tf_op jit(solution)/shard_map/all_to_all | solution.py:71
  44.1 65.7 %copy-start.5 = (bf16[1,128,384]{2,1,0:T(8,128)(2,1)S(1)}, bf16[1,128,384]{2,1,0:T(8,128)(2,1)}, u32[]{:S(2)}) copy-start(bf16[1,128,384]{2,1,0:T(8,128)(2,1)} %param.11) | copy-start | bytes 294916
  103.5 91.4 %all-to-all-start = ((bf16[64,18,1024]{2,1,0:T(8,128)(2,1)}), bf16[64,18,1024]{2,1,0:T(8,128)(2,1)}, u32[]{:S(2)}, u32[]{:S(2)}) async-start(bf16[64,18,1024]{2,1,0:T(8,128)(2,1)} %reshape.73), calls=%async_computation | async-start | bytes 6291456 | tf_op jit(solution)/shard_map/all_to_all | solution.py:72
  197.9 3.4 %copy-start.4 = (bf16[1,384,1024]{2,1,0:T(8,128)(2,1)S(1)}, bf16[1,384,1024]{2,1,0:T(8,128)(2,1)}, u32[]{:S(2)}) copy-start(bf16[1,384,1024]{2,1,0:T(8,128)(2,1)} %all_gather.9) | copy-start | bytes 2359300
  197.9 3.4 %copy-start.7 = (f32[1152,768]{0,1:T(8,128)S(1)}, f32[1152,768]{0,1:T(8,128)}, u32[]{:S(2)}) copy-start(f32[1152,768]{0,1:T(8,128)} %fusion.10) | copy-start | bytes 10616836
  201.4 1.7 copy-start.1
  203.0 3.4 %copy-start.2 = (bf16[1,1024,384]{2,1,0:T(8,128)(2,1)S(1)}, bf16[1,1024,384]{2,1,0:T(8,128)(2,1)}, u32[]{:S(2)}) copy-start(bf16[1,1024,384]{2,1,0:T(8,128)(2,1)} %all_gather.10) | copy-start | bytes 2359300
  203.0 3.4 %copy-start.3 = (bf16[1,1024,384]{2,1,0:T(8,128)(2,1)S(1)}, bf16[1,1024,384]{2,1,0:T(8,128)(2,1)}, u32[]{:S(2)}) copy-start(bf16[1,1024,384]{2,1,0:T(8,128)(2,1)} %all_gather.11) | copy-start | bytes 2359300
  210.9 97.1 %all-to-all-start.2 = ((bf16[64,18,1024]{2,1,0:T(8,128)(2,1)}), bf16[64,18,1024]{2,1,0:T(8,128)(2,1)}, u32[]{:S(2)}, u32[]{:S(2)}) async-start(bf16[64,18,1024]{2,1,0:T(8,128)(2,1)} %reshape.78), calls=%async_computation.2 | async-start | bytes 6291456 | tf_op jit(solution)/shard_map/all_to_all | solution.py:77
  234.5 85.5 %reduce-scatter.4.cloned.1.call-start = ((), (), s32[]{:S(2)}) async-start(), calls=%async_computation.4 | async-start | bytes 2654208
Sparse Core Ops, SparseCore 0:
  239.1 41.3 reduce-scatter.3
where the time goes:
time: 331 us; the launch traced here: 330 us
  waiting for transfers between devices  128 us (39%)
  blocking collectives  76.9 us (23%)
  starting transfers between devices  41.9 us (13%)
  local copies, waits for them, and re-layouts  35.2 us (11%)
  other arithmetic  17.1 us (5%)
  matrix products  16.7 us (5%)
  between operations  14.2 us (4%)
    all_to_all x1, waiting for transfers between devices, body(): lax.all_to_all(d_rows.reshape(experts, capacity, model_width), 'expert',...  68.9 us
    all_to_all x1, waiting for transfers between devices, body(): lax.all_to_all(send_inputs, 'expert', split_axis=0, concat_axis=0, tiled=...  59.5 us
    all_gather x1, blocking collectives, body(): lax.all_gather(gate_weight, 'dp', axis=1, tiled=True)  30.3 us
    all_gather x1, blocking collectives, body(): lax.all_gather(up_weight, 'dp', axis=1, tiled=True)  24.1 us
    all_to_all x1, starting transfers between devices, body(): lax.all_to_all(d_rows.reshape(experts, capacity, model_width), 'expert',...  23.6 us
    all_gather x1, blocking collectives, body(): lax.all_gather(down_weight, 'dp', axis=2, tiled=True)  22.5 us
    all_to_all x1, starting transfers between devices, body(): lax.all_to_all(send_inputs, 'expert', split_axis=0, concat_axis=0, tiled=...  11.8 us
    scatter x1, other arithmetic, body(): send_grads = jnp.zeros((slot_count, model_width), jnp.bfloat16).at[positi...  7.72 us
  transfers between devices with their start and end apart: 4, of which 2 were waited for; matrix products, arithmetic and copies ran while one was open for 12% of the time, Pallas kernels for 0%

commit v1 on v0

--- a/solution.py
+++ b/solution.py
@@ -2,6 +2,13 @@
 import jax.numpy as jnp
 from jax import lax
 from jax.sharding import PartitionSpec as P
+
+
+def exchange_gather(block, name, dim):
+    count = lax.axis_size(name)
+    blocks = jnp.stack([block for _ in range(count)])
+    blocks = lax.all_to_all(blocks, name, split_axis=0, concat_axis=0)
+    return jnp.concatenate(blocks, axis=dim)
 
 
 def route_slots(routes, experts):
@@ -62,7 +69,7 @@
     whole_gate, whole_up, whole_down = (
         lax.all_gather(gate_weight, "dp", axis=1, tiled=True),
         lax.all_gather(up_weight, "dp", axis=1, tiled=True),
-        lax.all_gather(down_weight, "dp", axis=2, tiled=True),
+        exchange_gather(down_weight, "dp", 2),
     )
     gate_up = jnp.concatenate([whole_gate[0], whole_up[0]], axis=1)
     down_matrix = whole_down[0]

time: 331 us -> 395 us (1.19)
  waiting for transfers between devices: 128 us -> 204 us
  blocking collectives: 76.9 us -> 60.8 us
  local copies, waits for them, and re-layouts: 35.2 us -> 40.6 us
    all_to_all x1, waiting for transfers between devices: 0.01 us -> 62.2 us  [body(): lax.all_to_all(send_grads, 'expert', split_axis=0, concat_axis=0, tiled=T...]
    all_gather x1 -> x0, blocking collectives: 22.5 us -> none  [body(): lax.all_gather(down_weight, 'dp', axis=2, tiled=True)]
    all_to_all x1, waiting for transfers between devices: 59.5 us -> 72.4 us  [body(): lax.all_to_all(send_inputs, 'expert', split_axis=0, concat_axis=0, tiled=...]
    all_to_all x0 -> x1, starting transfers between devices: none -> 10.2 us  [exchange_gather(): blocks = lax.all_to_all(blocks, name, split_axis=0, concat_axis=0)]
    all_to_all x1, starting transfers between devices: 23.6 us -> 16.3 us  [body(): lax.all_to_all(d_rows.reshape(experts, capacity, model_width), 'expert',...]
    all_gather x1, blocking collectives: 30.3 us -> 37.3 us  [body(): lax.all_gather(gate_weight, 'dp', axis=1, tiled=True)]
    all_to_all x1, starting transfers between devices: 11.8 us -> 6.25 us  [body(): lax.all_to_all(send_inputs, 'expert', split_axis=0, concat_axis=0, tiled=...]
    all_to_all x1, starting transfers between devices: 6.25 us -> 11.6 us  [body(): lax.all_to_all(send_grads, 'expert', split_axis=0, concat_axis=0, tiled=T...]
  transfers between devices with their start and end apart: 4 -> 5, of which waited for: 2 -> 3; matrix products, arithmetic and copies ran while one was open for 12% -> 10% of each run, Pallas kernels for 0% -> 0%
where the time goes in v1:
time: 395 us; the launch traced here: 394 us
  waiting for transfers between devices  204 us (52%)
  blocking collectives  60.8 us (15%)
  starting transfers between devices  44.6 us (11%)
  local copies, waits for them, and re-layouts  40.6 us (10%)
  other arithmetic  15 us (4%)
  matrix products  15 us (4%)
  between operations  14.2 us (4%)
    all_to_all x1, waiting for transfers between devices, body(): lax.all_to_all(send_inputs, 'expert', split_axis=0, concat_axis=0, tiled=...  72.4 us
    all_to_all x1, waiting for transfers between devices, body(): lax.all_to_all(d_rows.reshape(experts, capacity, model_width), 'expert',...  68.9 us
    all_to_all x1, waiting for transfers between devices, body(): lax.all_to_all(send_grads, 'expert', split_axis=0, concat_axis=0, tiled=T...  62.2 us
    all_gather x1, blocking collectives, body(): lax.all_gather(gate_weight, 'dp', axis=1, tiled=True)  37.3 us
    all_gather x1, blocking collectives, body(): lax.all_gather(up_weight, 'dp', axis=1, tiled=True)  23.6 us
    all_to_all x1, starting transfers between devices, body(): lax.all_to_all(d_rows.reshape(experts, capacity, model_width), 'expert',...  16.3 us
    all_to_all x1, starting transfers between devices, body(): lax.all_to_all(send_grads, 'expert', split_axis=0, concat_axis=0, tiled=T...  11.6 us
    all_to_all x1, starting transfers between devices, exchange_gather(): blocks = lax.all_to_all(blocks, name, split_axis=0, concat_axis=0)  10.2 us
  transfers between devices with their start and end apart: 5, of which 3 were waited for; matrix products, arithmetic and copies ran while one was open for 10% of the time, Pallas kernels for 0%

profile of v1, /device:TPU:1, one launch (start us, length us, event | category | flops | bytes accessed | tf_op | source)
XLA Modules:
  0.0 393.8 jit_solution(10095301421623919974)
XLA Ops:
  10.7 1.0 convert_element_type.34
  11.7 6.4 %scatter_custom_fusion = bf16[1152,1024]{1,0:T(8,128)(2,1)S(1)} fusion(s32[1024]{0:T(1024)S(1)} %bitcast.40, f32[128,1024]{1,0:T(8,128)S(1)} %convert_element_type.34, f32[1024]{0:T(1024)S(1)} %mul.60, bf16[]{:T(256)} %constant.6.clone.1), kind=kCustom, calls=%fused_computation.7 | custom fusion | flops 2097152 | bytes 2887682 | tf_op jit(solution)/shard_map/scatter | solution.py:66
  18.1 2.4 reshape.79
  20.5 11.6 %all-to-all-start = ((bf16[64,18,1024]{2,1,0:T(8,128)(2,1)}), bf16[64,18,1024]{2,1,0:T(8,128)(2,1)S(1)}, u32[]{:S(2)}, u32[]{:S(2)}) async-start(bf16[64,18,1024]{2,1,0:T(8,128)(2,1)} %reshape.79), calls=%async_computation | async-start | bytes 6291456 | tf_op jit(solution)/shard_map/all_to_all | solution.py:79
  32.2 7.0 %scatter_custom_fusion.1 = bf16[1152,1024]{1,0:T(8,128)(2,1)} fusion(s32[1024]{0:T(1024)S(1)} %bitcast.41, bf16[]{:T(256)} %constant.6.clone.1, bf16[128,1024]{1,0:T(8,128)(2,1)S(1)} %copy-done), kind=kCustom, calls=%fused_computation.9 | custom fusion | bytes 2621442 | tf_op jit(solution)/shard_map/scatter | solution.py:60
  39.2 4.3 %reshape.83 = bf16[64,18,1024]{2,1,0:T(8,128)(2,1)} reshape(bf16[1152,1024]{1,0:T(8,128)(2,1)} %scatter_custom_fusion.1) | data formatting | bytes 4718592 | tf_op jit(solution)/shard_map/reshape | solution.py:61
  43.5 62.2 %all-to-all-done = bf16[64,18,1024]{2,1,0:T(8,128)(2,1)S(1)} async-done(((bf16[64,18,1024]{2,1,0:T(8,128)(2,1)}), bf16[64,18,1024]{2,1,0:T(8,128)(2,1)S(1)}, u32[]{:S(2)}, u32[]{:S(2)}) %all-to-all-start) | async-done | bytes 2359328 | tf_op jit(solution)/shard_map/all_to_all | solution.py:79
  105.7 6.2 %all-to-all-start.2 = ((bf16[64,18,1024]{2,1,0:T(8,128)(2,1)}), bf16[64,18,1024]{2,1,0:T(8,128)(2,1)}, u32[]{:S(2)}, u32[]{:S(2)}) async-start(bf16[64,18,1024]{2,1,0:T(8,128)(2,1)} %reshape.83), calls=%async_computation.2 | async-start | bytes 6291456 | tf_op jit(solution)/shard_map/all_to_all | solution.py:78
  111.9 1.0 copy.32
  112.9 72.4 %all-to-all-done.2 = bf16[64,18,1024]{2,1,0:T(8,128)(2,1)} async-done(((bf16[64,18,1024]{2,1,0:T(8,128)(2,1)}), bf16[64,18,1024]{2,1,0:T(8,128)(2,1)}, u32[]{:S(2)}, u32[]{:S(2)}) %all-to-all-start.2) | async-done | bytes 2359328 | tf_op jit(solution)/shard_map/all_to_all | solution.py:78
  185.4 1.0 stack.2
  186.3 10.2 %all-to-all-start.1 = ((bf16[8,1,384,128]{2,3,1,0:T(8,128)(2,1)}), bf16[8,1,384,128]{2,3,1,0:T(8,128)(2,1)}, u32[]{:S(2)}, u32[]{:S(2)}) async-start(bf16[8,1,384,128]{2,3,1,0:T(8,128)(2,1)} %stack.2), calls=%async_computation.1 | async-start | bytes 1572864 | tf_op jit(solution)/shard_map/all_to_all | solution.py:10
  196.5 37.3 %all_gather.6 = bf16[1,1024,384]{2,1,0:T(8,128)(2,1)} all-gather(bf16[1,128,384]{2,1,0:T(8,128)(2,1)} %param.11), channel_id=1, replica_groups=mesh['dp'=8,'expert'=64] {'dp'}, dimensions={1}, use_global_device_ids=true | all-gather | bytes 884736 | tf_op jit(solution)/shard_map/all_gather | solution.py:70
  233.8 23.6 %all_gather.7 = bf16[1,1024,384]{2,1,0:T(8,128)(2,1)} all-gather(bf16[1,128,384]{2,1,0:T(8,128)(2,1)S(1)} %copy-done.5), channel_id=1, replica_groups=mesh['dp'=8,'expert'=64] {'dp'}, dimensions={1}, use_global_device_ids=true | all-gather | bytes 884736 | tf_op jit(solution)/shard_map/all_gather | solution.py:71
  257.3 2.3 reshape.80
  259.6 3.0 reshape.84
  262.6 3.5 fusion.10
  266.2 1.7 copy-done.6
  267.9 1.2 convolution_convert_fusion.2
  269.2 4.7 %multiply_convert_fusion.2 = (bf16[1152,384]{0,1:T(8,128)(2,1)S(1)}, bf16[1152,384]{0,1:T(8,128)(2,1)S(1)}) fusion(f32[1152,768]{0,1:T(8,128)} %copy-done.6, bf16[1152,1024]{1,0:T(8,128)(2,1)} %reshape.80, bf16[384,1024]{0,1:T(8,128)(2,1)} %bitcast.5), kind=kOutput, calls=%fused_computation.16 | convolution fusion | flops 911720448 | bytes 8454144 | tf_op jit(solution)/shard_map/dot_general | solution.py:34
  273.9 3.3 convolution_convert_fusion.1
  277.2 2.1 convolution_convert_fusion
  279.3 2.4 reshape.85
  281.7 16.3 %all-to-all-start.3 = ((bf16[64,18,1024]{2,1,0:T(8,128)(2,1)}), bf16[64,18,1024]{2,1,0:T(8,128)(2,1)}, u32[]{:S(2)}, u32[]{:S(2)}) async-start(bf16[64,18,1024]{2,1,0:T(8,128)(2,1)} %reshape.85), calls=%async_computation.3 | async-start | bytes 6291456 | tf_op jit(solution)/shard_map/all_to_all | solution.py:84
  298.2 1.6 pad_maximum_fusion
  299.8 2.6 copy.36
  302.5 68.9 %all-to-all-done.3 = bf16[64,18,1024]{2,1,0:T(8,128)(2,1)} async-done(((bf16[64,18,1024]{2,1,0:T(8,128)(2,1)}), bf16[64,18,1024]{2,1,0:T(8,128)(2,1)}, u32[]{:S(2)}, u32[]{:S(2)}) %all-to-all-start.3) | async-done | bytes 2359328 | tf_op jit(solution)/shard_map/all_to_all | solution.py:84
  371.4 2.9 reshape.86
  374.3 5.3 %gather_fusion = bf16[1024,1024]{1,0:T(8,128)(2,1)} fusion(bf16[1152,1024]{1,0:T(8,128)(2,1)S(1)} %reshape.86, s32[1024]{0:T(1024)S(1)} %broadcast_clamp_fusion), kind=kCustom, calls=%fused_computation | custom fusion | bytes 4198400 | tf_op jit(solution)/shard_map/gather | solution.py:91
  379.7 3.7 bitcast_reduce_fusion
  383.4 1.2 copy.37
  385.4 0.8 copy.35
  (31 shorter events, 5.4 us)
Async XLA Ops:
  7.2 25.0 %copy-start = (bf16[128,1024]{1,0:T(8,128)(2,1)S(1)}, bf16[128,1024]{1,0:T(8,128)(2,1)}, u32[]{:S(2)}) copy-start(bf16[128,1024]{1,0:T(8,128)(2,1)} %param.7) | copy-start | bytes 786436
  20.5 85.1 %all-to-all-start = ((bf16[64,18,1024]{2,1,0:T(8,128)(2,1)}), bf16[64,18,1024]{2,1,0:T(8,128)(2,1)S(1)}, u32[]{:S(2)}, u32[]{:S(2)}) async-start(bf16[64,18,1024]{2,1,0:T(8,128)(2,1)} %reshape.79), calls=%async_computation | async-start | bytes 6291456 | tf_op jit(solution)/shard_map/all_to_all | solution.py:79
  105.7 79.7 %all-to-all-start.2 = ((bf16[64,18,1024]{2,1,0:T(8,128)(2,1)}), bf16[64,18,1024]{2,1,0:T(8,128)(2,1)}, u32[]{:S(2)}, u32[]{:S(2)}) async-start(bf16[64,18,1024]{2,1,0:T(8,128)(2,1)} %reshape.83), calls=%async_computation.2 | async-start | bytes 6291456 | tf_op jit(solution)/shard_map/all_to_all | solution.py:78
  186.3 47.4 %copy-start.5 = (bf16[1,128,384]{2,1,0:T(8,128)(2,1)S(1)}, bf16[1,128,384]{2,1,0:T(8,128)(2,1)}, u32[]{:S(2)}) copy-start(bf16[1,128,384]{2,1,0:T(8,128)(2,1)} %param.12) | copy-start | bytes 294916
  186.3 82.8 %all-to-all-start.1 = ((bf16[8,1,384,128]{2,3,1,0:T(8,128)(2,1)}), bf16[8,1,384,128]{2,3,1,0:T(8,128)(2,1)}, u32[]{:S(2)}, u32[]{:S(2)}) async-start(bf16[8,1,384,128]{2,3,1,0:T(8,128)(2,1)} %stack.2), calls=%async_computation.1 | async-start | bytes 1572864 | tf_op jit(solution)/shard_map/all_to_all | solution.py:10
  259.6 3.0 copy-start.2
  262.6 5.3 %copy-start.1 = (bf16[1152,1024]{1,0:T(8,128)(2,1)S(1)}, bf16[1152,1024]{1,0:T(8,128)(2,1)}, u32[]{:S(2)}) copy-start(bf16[1152,1024]{1,0:T(8,128)(2,1)} %reshape.80) | copy-start | bytes 7077892
  266.2 1.8 copy-start.6
  273.8 3.4 copy-start.3
  273.8 3.4 copy-start.4
  281.7 89.7 %all-to-all-start.3 = ((bf16[64,18,1024]{2,1,0:T(8,128)(2,1)}), bf16[64,18,1024]{2,1,0:T(8,128)(2,1)}, u32[]{:S(2)}, u32[]{:S(2)}) async-start(bf16[64,18,1024]{2,1,0:T(8,128)(2,1)} %reshape.85), calls=%async_computation.3 | async-start | bytes 6291456 | tf_op jit(solution)/shard_map/all_to_all | solution.py:84
  297.9 85.5 %reduce-scatter.4.cloned.1.call-start = ((), (), s32[]{:S(2)}) async-start(), calls=%async_computation.5 | async-start | bytes 2654208
Sparse Core Ops, SparseCore 0:
  302.6 42.2 reduce-scatter.3
